TPU v7x, 256 devices: a whole 4x4x8 slice. The times are simulated.
256 devices in a mesh: section: 16 (over x, y), col: 16 (over z, core).
Axes of the slice: x: 4, y: 4, z: 8, core: 2. Of those that a mesh axis runs over, the one named last changes fastest.
Arguments:
- features: bfloat16 [4, 32, 65536], P(None, 'section', 'col'), may hold values from -48 to 48
- weights: bfloat16 [16, 512, 4, 128, 128], P('section', 'col'), may hold values from -0.375 to 0.375
- sources: int32 [16, 512, 4], P('section', 'col'), may hold values from 0 to 511, as said below
- bias: float32 [16, 65536], P('section', 'col'), may hold values from -0.3 to 0.3
- batch_rows: int32 [4], replicated, may hold values from 1 to 32, as said below
Outputs:
- final_act: bfloat16 [4, 32, 65536], P(None, 'section', 'col')
Inputs may be any that keep to these rules, and one draw needn't show every extreme that they name: In every layer, the sources of all block columns c with c // 32 = d name exactly 2 distinct blocks b with b // 32 = e, for every pair d, e. `batch_rows`: some micro-batch has exactly 32 live rows.
All inputs are finite; a program needn't handle non-finite values.
Results may differ from a plain program's by a relative error of at most 0.033.
Values may be sent and summed in bfloat16 or wider, within the bound.
A program may use at most 64 MiB of HBM per device.

v0:
```python
import jax
import jax.numpy as jnp
from jax import lax
from jax.sharding import PartitionSpec as P

CAP = 2


def from_behind(x, axis, by):
    size = lax.axis_size(axis)
    pairs = [(i, i + by) for i in range(size) if 0 <= i + by < size]
    return lax.ppermute(x, axis, pairs)


def request_lists(pattern_table, owners, blocks_own, slot_total):
    dest_entries = pattern_table.reshape(owners, -1)
    block_total = owners * blocks_own
    catalog = jnp.arange(block_total, dtype=jnp.int32)
    wanted = jnp.any(dest_entries[:, :, None] == catalog[None, None, :], axis=1)
    wanted = wanted.reshape(owners, owners, blocks_own)
    block_ranks = jnp.cumsum(wanted.astype(jnp.int32), axis=2) - 1
    slot_ids = jnp.arange(slot_total, dtype=jnp.int32)
    chosen = wanted[:, :, None, :] & (block_ranks[:, :, None, :] == slot_ids[None, None, :, None])
    local_ids = jnp.arange(blocks_own, dtype=jnp.int32)
    positions = jnp.sum(chosen.astype(jnp.int32) * local_ids[None, None, None, :], axis=3)
    present = jnp.any(chosen, axis=3)
    return (positions, present)


def body(features, weights, sources, bias, batch_rows):
    sections = lax.axis_size("section")
    owners = lax.axis_size("col")
    section_idx = lax.axis_index("section")
    col_idx = lax.axis_index("col")
    local_w = weights[0]
    blocks_own = local_w.shape[0]
    nonzero_count = local_w.shape[1]
    block_size = local_w.shape[2]
    local_src = sources[0].reshape(blocks_own * nonzero_count)
    local_bias = bias[0].reshape(blocks_own, 1, block_size)
    pattern_table = lax.all_gather(sources[0], "col", axis=0, tiled=True)
    positions, present = request_lists(pattern_table, owners, blocks_own, CAP)
    outgoing = lax.dynamic_index_in_dim(positions, col_idx, 1, keepdims=False).reshape(owners * CAP)
    incoming = lax.dynamic_index_in_dim(positions, col_idx, 0, keepdims=False)
    incoming_ok = lax.dynamic_index_in_dim(present, col_idx, 0, keepdims=False)
    global_ids = incoming + blocks_own * jnp.arange(owners, dtype=jnp.int32)[:, None]
    matches = (local_src[:, None] == global_ids.reshape(-1)[None, :]) & incoming_ok.reshape(-1)[
        None, :
    ]
    slot_of = jnp.sum(
        matches.astype(jnp.int32) * jnp.arange(owners * CAP, dtype=jnp.int32)[None, :], axis=1
    )
    all_inputs = lax.all_gather(features, "section", axis=1, tiled=True)
    batches = all_inputs.shape[0]
    row_total = all_inputs.shape[1]
    pieces = 1
    part_rows = row_total // pieces
    piece_total = batches * pieces
    tick_total = piece_total + sections - 1
    blocks_in = all_inputs.reshape(batches, pieces, part_rows, blocks_own, block_size)
    blocks_in = blocks_in.transpose(0, 1, 3, 2, 4).reshape(
        piece_total, blocks_own, part_rows, block_size
    )

    def combine(received):
        rows_here = received.shape[2]
        flat_recv = received.reshape(owners * CAP, rows_here, block_size)
        picked = jnp.take(flat_recv, slot_of, axis=0).reshape(
            blocks_own, nonzero_count, rows_here, block_size
        )
        preact = jnp.einsum("ckrb,ckbo->cro", picked, local_w, preferred_element_type=jnp.float32)
        return jnp.clip(preact + local_bias, 0.0, 32.0).astype(jnp.bfloat16)

    def apply_layer(carried):
        payload = jnp.take(carried, outgoing, axis=0).reshape(
            owners, CAP, carried.shape[1], block_size
        )
        return combine(lax.all_to_all(payload, "col", split_axis=0, concat_axis=0, tiled=True))

    def tick(tick_idx, carry):
        carried, finished = carry
        entering = lax.dynamic_index_in_dim(
            blocks_in, jnp.minimum(tick_idx, piece_total - 1), 0, keepdims=False
        )
        current = jnp.where(section_idx == 0, entering, carried)
        layer_out = apply_layer(current)
        slot_idx = jnp.clip(tick_idx - sections + 1, 0, piece_total - 1)
        storing = (section_idx == sections - 1) & (tick_idx >= sections - 1)
        existing = lax.dynamic_index_in_dim(finished, slot_idx, 0, keepdims=False)
        finished = lax.dynamic_update_index_in_dim(
            finished, jnp.where(storing, layer_out, existing), slot_idx, 0
        )
        passed = from_behind(layer_out, "section", 1)
        return (passed, finished)

    initial = (
        jnp.zeros((blocks_own, part_rows, block_size), jnp.bfloat16),
        jnp.zeros((piece_total, blocks_own, part_rows, block_size), jnp.bfloat16),
    )
    carried, finished = lax.fori_loop(0, tick_total, tick, initial)
    completed = finished.reshape(batches, pieces, blocks_own, part_rows, block_size)
    completed = completed.transpose(0, 1, 3, 2, 4).reshape(
        batches, row_total, blocks_own * block_size
    )
    own_rows = row_total // sections
    outgoing_rows = completed.reshape(batches, sections, own_rows, blocks_own * block_size)
    gathered = lax.all_to_all(outgoing_rows, "section", split_axis=1, concat_axis=1, tiled=True)
    own_result = gathered[:, sections - 1]
    row_ids = section_idx * own_rows + jnp.arange(own_rows, dtype=jnp.int32)
    row_mask = row_ids[None, :] < batch_rows[:, None]
    return jnp.where(row_mask[:, :, None], own_result, jnp.zeros_like(own_result))


def solution(mesh):
    in_specs = (
        P(None, "section", "col"),
        P("section", "col", None, None, None),
        P("section", "col", None),
        P("section", "col"),
        P(),
    )
    out_specs = P(None, "section", "col")
    return jax.shard_map(body, mesh=mesh, in_specs=in_specs, out_specs=out_specs, check_vma=False)
```

profile of v0, /device:TPU:8, one launch (start us, length us, event | category | flops | bytes accessed | tf_op | source)
XLA Modules:
  0.0 745.7 jit_solution(5742801372019623297)
XLA Ops:
  9.9 20.7 %all-gather = s32[1,512,4]{2,0,1:T(1,128)S(1)} all-gather(s32[1,32,4]{2,0,1:T(1,128)S(1)} %copy.19), channel_id=2, replica_groups=mesh['section'=16,'col'=16] {'col'}, dimensions={1}, use_global_device_ids=true | all-gather | bytes 8704 | tf_op jit(solution)/shard_map/all_gather | solution.py:41
  38.9 21.1 %all-gather.3.cloned.1.call-done = bf16[4,32,4096]{2,0,1:T(4,128)(2,1)} async-done(((bf16[4,2,4096]{2,0,1:T(4,128)(2,1)}), bf16[4,32,4096]{2,0,1:T(4,128)(2,1)}) %all-gather.3.cloned.1.call-update) | async-done | bytes 1048592 | tf_op jit(solution)/shard_map/all_gather | solution.py:53
  63.2 641.0 %while.19 = (s32[]{:T(128)}, bf16[32,32,128]{2,1,0:T(8,128)(2,1)S(1)}, bf16[4,32,32,128]{3,2,1,0:T(8,128)(2,1)S(1)}, s32[128]{0:T(128)S(1)}, s32[32]{0:T(128)S(1...) while((s32[]{:T(128)}, ...), condition=%wide.region_6.7_spmd, body=%wide.region_5.6_spmd.sunk | while | flops 135531952 | bytes 12878729 | solution.py:100
  65.9 7.1 all-to-all-start
  73.2 11.0 %all-to-all-done = bf16[16,2,32,128]{3,2,1,0:T(8,128)(2,1)S(1)} async-done(((bf16[16,2,32,128]{3,2,1,0:T(8,128)(2,1)}), bf16[16,2,32,128]{3,2,1,0:T(8,128)(2,1)S(1)}, u32[]{:S(2)}, u32[]{:S(2)}) %all-to-all-start) | async-done | bytes 262176 | tf_op jit(solution)/shard_map/while/body/eval_jaxpr/all_to_all | solution.py:78
  91.2 7.8 %collective-permute-done = bf16[32,32,128]{2,1,0:T(8,128)(2,1)S(1)} collective-permute-done((bf16[32,32,128]{2,1,0:T(8,128)(2,1)S(1)}, bf16[32,32,128]{2,1,0:T(8,128)(2,1)S(1)}, u32[]{:S(2)}, u32[]{:S(2)}) %collective-permute-start) | collective-permute-done | bytes 262176 | tf_op jit(solution)/shard_map/while/body/eval_jaxpr/ppermute | solution.py:12
  105.4 10.8 %all-to-all-done = bf16[16,2,32,128]{3,2,1,0:T(8,128)(2,1)S(1)} async-done(((bf16[16,2,32,128]{3,2,1,0:T(8,128)(2,1)}), bf16[16,2,32,128]{3,2,1,0:T(8,128)(2,1)S(1)}, u32[]{:S(2)}, u32[]{:S(2)}) %all-to-all-start) | async-done | bytes 262176 | tf_op jit(solution)/shard_map/while/body/eval_jaxpr/all_to_all | solution.py:78
  123.3 7.7 %collective-permute-done = bf16[32,32,128]{2,1,0:T(8,128)(2,1)S(1)} collective-permute-done((bf16[32,32,128]{2,1,0:T(8,128)(2,1)S(1)}, bf16[32,32,128]{2,1,0:T(8,128)(2,1)S(1)}, u32[]{:S(2)}, u32[]{:S(2)}) %collective-permute-start) | collective-permute-done | bytes 262176 | tf_op jit(solution)/shard_map/while/body/eval_jaxpr/ppermute | solution.py:12
  137.3 10.8 %all-to-all-done = bf16[16,2,32,128]{3,2,1,0:T(8,128)(2,1)S(1)} async-done(((bf16[16,2,32,128]{3,2,1,0:T(8,128)(2,1)}), bf16[16,2,32,128]{3,2,1,0:T(8,128)(2,1)S(1)}, u32[]{:S(2)}, u32[]{:S(2)}) %all-to-all-start) | async-done | bytes 262176 | tf_op jit(solution)/shard_map/while/body/eval_jaxpr/all_to_all | solution.py:78
  155.2 7.7 %collective-permute-done = bf16[32,32,128]{2,1,0:T(8,128)(2,1)S(1)} collective-permute-done((bf16[32,32,128]{2,1,0:T(8,128)(2,1)S(1)}, bf16[32,32,128]{2,1,0:T(8,128)(2,1)S(1)}, u32[]{:S(2)}, u32[]{:S(2)}) %collective-permute-start) | collective-permute-done | bytes 262176 | tf_op jit(solution)/shard_map/while/body/eval_jaxpr/ppermute | solution.py:12
  169.3 10.8 %all-to-all-done = bf16[16,2,32,128]{3,2,1,0:T(8,128)(2,1)S(1)} async-done(((bf16[16,2,32,128]{3,2,1,0:T(8,128)(2,1)}), bf16[16,2,32,128]{3,2,1,0:T(8,128)(2,1)S(1)}, u32[]{:S(2)}, u32[]{:S(2)}) %all-to-all-start) | async-done | bytes 262176 | tf_op jit(solution)/shard_map/while/body/eval_jaxpr/all_to_all | solution.py:78
  187.2 7.6 %collective-permute-done = bf16[32,32,128]{2,1,0:T(8,128)(2,1)S(1)} collective-permute-done((bf16[32,32,128]{2,1,0:T(8,128)(2,1)S(1)}, bf16[32,32,128]{2,1,0:T(8,128)(2,1)S(1)}, u32[]{:S(2)}, u32[]{:S(2)}) %collective-permute-start) | collective-permute-done | bytes 262176 | tf_op jit(solution)/shard_map/while/body/eval_jaxpr/ppermute | solution.py:12
  201.2 10.8 %all-to-all-done = bf16[16,2,32,128]{3,2,1,0:T(8,128)(2,1)S(1)} async-done(((bf16[16,2,32,128]{3,2,1,0:T(8,128)(2,1)}), bf16[16,2,32,128]{3,2,1,0:T(8,128)(2,1)S(1)}, u32[]{:S(2)}, u32[]{:S(2)}) %all-to-all-start) | async-done | bytes 262176 | tf_op jit(solution)/shard_map/while/body/eval_jaxpr/all_to_all | solution.py:78
  234.0 10.8 %all-to-all-done = bf16[16,2,32,128]{3,2,1,0:T(8,128)(2,1)S(1)} async-done(((bf16[16,2,32,128]{3,2,1,0:T(8,128)(2,1)}), bf16[16,2,32,128]{3,2,1,0:T(8,128)(2,1)S(1)}, u32[]{:S(2)}, u32[]{:S(2)}) %all-to-all-start) | async-done | bytes 262176 | tf_op jit(solution)/shard_map/while/body/eval_jaxpr/all_to_all | solution.py:78
  248.7 6.5 collective-permute-start
  268.0 10.8 %all-to-all-done = bf16[16,2,32,128]{3,2,1,0:T(8,128)(2,1)S(1)} async-done(((bf16[16,2,32,128]{3,2,1,0:T(8,128)(2,1)}), bf16[16,2,32,128]{3,2,1,0:T(8,128)(2,1)S(1)}, u32[]{:S(2)}, u32[]{:S(2)}) %all-to-all-start) | async-done | bytes 262176 | tf_op jit(solution)/shard_map/while/body/eval_jaxpr/all_to_all | solution.py:78
  282.7 6.5 collective-permute-start
  302.1 10.8 %all-to-all-done = bf16[16,2,32,128]{3,2,1,0:T(8,128)(2,1)S(1)} async-done(((bf16[16,2,32,128]{3,2,1,0:T(8,128)(2,1)}), bf16[16,2,32,128]{3,2,1,0:T(8,128)(2,1)S(1)}, u32[]{:S(2)}, u32[]{:S(2)}) %all-to-all-start) | async-done | bytes 262176 | tf_op jit(solution)/shard_map/while/body/eval_jaxpr/all_to_all | solution.py:78
  316.7 6.5 collective-permute-start
  336.1 10.8 %all-to-all-done = bf16[16,2,32,128]{3,2,1,0:T(8,128)(2,1)S(1)} async-done(((bf16[16,2,32,128]{3,2,1,0:T(8,128)(2,1)}), bf16[16,2,32,128]{3,2,1,0:T(8,128)(2,1)S(1)}, u32[]{:S(2)}, u32[]{:S(2)}) %all-to-all-start) | async-done | bytes 262176 | tf_op jit(solution)/shard_map/while/body/eval_jaxpr/all_to_all | solution.py:78
  370.2 10.8 %all-to-all-done = bf16[16,2,32,128]{3,2,1,0:T(8,128)(2,1)S(1)} async-done(((bf16[16,2,32,128]{3,2,1,0:T(8,128)(2,1)}), bf16[16,2,32,128]{3,2,1,0:T(8,128)(2,1)S(1)}, u32[]{:S(2)}, u32[]{:S(2)}) %all-to-all-start) | async-done | bytes 262176 | tf_op jit(solution)/shard_map/while/body/eval_jaxpr/all_to_all | solution.py:78
  404.2 10.8 %all-to-all-done = bf16[16,2,32,128]{3,2,1,0:T(8,128)(2,1)S(1)} async-done(((bf16[16,2,32,128]{3,2,1,0:T(8,128)(2,1)}), bf16[16,2,32,128]{3,2,1,0:T(8,128)(2,1)S(1)}, u32[]{:S(2)}, u32[]{:S(2)}) %all-to-all-start) | async-done | bytes 262176 | tf_op jit(solution)/shard_map/while/body/eval_jaxpr/all_to_all | solution.py:78
  438.2 10.8 %all-to-all-done = bf16[16,2,32,128]{3,2,1,0:T(8,128)(2,1)S(1)} async-done(((bf16[16,2,32,128]{3,2,1,0:T(8,128)(2,1)}), bf16[16,2,32,128]{3,2,1,0:T(8,128)(2,1)S(1)}, u32[]{:S(2)}, u32[]{:S(2)}) %all-to-all-start) | async-done | bytes 262176 | tf_op jit(solution)/shard_map/while/body/eval_jaxpr/all_to_all | solution.py:78
  472.3 10.8 %all-to-all-done = bf16[16,2,32,128]{3,2,1,0:T(8,128)(2,1)S(1)} async-done(((bf16[16,2,32,128]{3,2,1,0:T(8,128)(2,1)}), bf16[16,2,32,128]{3,2,1,0:T(8,128)(2,1)S(1)}, u32[]{:S(2)}, u32[]{:S(2)}) %all-to-all-start) | async-done | bytes 262176 | tf_op jit(solution)/shard_map/while/body/eval_jaxpr/all_to_all | solution.py:78
  506.3 10.8 %all-to-all-done = bf16[16,2,32,128]{3,2,1,0:T(8,128)(2,1)S(1)} async-done(((bf16[16,2,32,128]{3,2,1,0:T(8,128)(2,1)}), bf16[16,2,32,128]{3,2,1,0:T(8,128)(2,1)S(1)}, u32[]{:S(2)}, u32[]{:S(2)}) %all-to-all-start) | async-done | bytes 262176 | tf_op jit(solution)/shard_map/while/body/eval_jaxpr/all_to_all | solution.py:78
  540.4 10.8 %all-to-all-done = bf16[16,2,32,128]{3,2,1,0:T(8,128)(2,1)S(1)} async-done(((bf16[16,2,32,128]{3,2,1,0:T(8,128)(2,1)}), bf16[16,2,32,128]{3,2,1,0:T(8,128)(2,1)S(1)}, u32[]{:S(2)}, u32[]{:S(2)}) %all-to-all-start) | async-done | bytes 262176 | tf_op jit(solution)/shard_map/while/body/eval_jaxpr/all_to_all | solution.py:78
  574.4 10.8 %all-to-all-done = bf16[16,2,32,128]{3,2,1,0:T(8,128)(2,1)S(1)} async-done(((bf16[16,2,32,128]{3,2,1,0:T(8,128)(2,1)}), bf16[16,2,32,128]{3,2,1,0:T(8,128)(2,1)S(1)}, u32[]{:S(2)}, u32[]{:S(2)}) %all-to-all-start) | async-done | bytes 262176 | tf_op jit(solution)/shard_map/while/body/eval_jaxpr/all_to_all | solution.py:78
  608.4 10.8 %all-to-all-done = bf16[16,2,32,128]{3,2,1,0:T(8,128)(2,1)S(1)} async-done(((bf16[16,2,32,128]{3,2,1,0:T(8,128)(2,1)}), bf16[16,2,32,128]{3,2,1,0:T(8,128)(2,1)S(1)}, u32[]{:S(2)}, u32[]{:S(2)}) %all-to-all-start) | async-done | bytes 262176 | tf_op jit(solution)/shard_map/while/body/eval_jaxpr/all_to_all | solution.py:78
  642.5 10.8 %all-to-all-done = bf16[16,2,32,128]{3,2,1,0:T(8,128)(2,1)S(1)} async-done(((bf16[16,2,32,128]{3,2,1,0:T(8,128)(2,1)}), bf16[16,2,32,128]{3,2,1,0:T(8,128)(2,1)S(1)}, u32[]{:S(2)}, u32[]{:S(2)}) %all-to-all-start) | async-done | bytes 262176 | tf_op jit(solution)/shard_map/while/body/eval_jaxpr/all_to_all | solution.py:78
  676.5 10.8 %all-to-all-done = bf16[16,2,32,128]{3,2,1,0:T(8,128)(2,1)S(1)} async-done(((bf16[16,2,32,128]{3,2,1,0:T(8,128)(2,1)}), bf16[16,2,32,128]{3,2,1,0:T(8,128)(2,1)S(1)}, u32[]{:S(2)}, u32[]{:S(2)}) %all-to-all-start) | async-done | bytes 262176 | tf_op jit(solution)/shard_map/while/body/eval_jaxpr/all_to_all | solution.py:78
  707.0 14.3 %all-to-all-start.1 = ((bf16[4,16,2,4096]{3,2,0,1:T(2,128)(2,1)}), bf16[4,16,2,4096]{3,2,0,1:T(2,128)(2,1)S(1)}, u32[]{:S(2)}, u32[]{:S(2)}) async-start(bf16[4,16,2,4096]{3,2,0,1:T(2,128)(2,1)} %copy.26), calls=%async_computation.1 | async-start | bytes 2097152 | tf_op jit(solution)/shard_map/all_to_all | solution.py:107
  721.5 16.6 %all-to-all-done.1 = bf16[4,16,2,4096]{3,2,0,1:T(2,128)(2,1)S(1)} async-done(((bf16[4,16,2,4096]{3,2,0,1:T(2,128)(2,1)}), bf16[4,16,2,4096]{3,2,0,1:T(2,128)(2,1)S(1)}, u32[]{:S(2)}, u32[]{:S(2)}) %all-to-all-start.1) | async-done | bytes 1048608 | tf_op jit(solution)/shard_map/all_to_all | solution.py:107
  (376 shorter events, 394.4 us)
Async XLA Ops:
  6.5 53.5 %all-gather.3.cloned.1.call-start = ((), (), s32[]{:S(2)}) async-start(), calls=%async_computation.2 | async-start | bytes 1114112 | tf_op jit(solution)/shard_map/all_gather | solution.py:53
  65.9 18.3 %all-to-all-start = ((bf16[16,2,32,128]{3,2,1,0:T(8,128)(2,1)}), bf16[16,2,32,128]{3,2,1,0:T(8,128)(2,1)S(1)}, u32[]{:S(2)}, u32[]{:S(2)}) async-start(bf16[16,2,32,128]{3,2,1,0:T(8,128)(2,1)} %broadcast_select_fusion.3), calls=%async_computation | async-start | bytes 524288 | tf_op jit(solution)/shard_map/while/body/eval_jaxpr/all_to_all | solution.py:78
  101.7 14.5 %all-to-all-start = ((bf16[16,2,32,128]{3,2,1,0:T(8,128)(2,1)}), bf16[16,2,32,128]{3,2,1,0:T(8,128)(2,1)S(1)}, u32[]{:S(2)}, u32[]{:S(2)}) async-start(bf16[16,2,32,128]{3,2,1,0:T(8,128)(2,1)} %broadcast_select_fusion.3), calls=%async_computation | async-start | bytes 524288 | tf_op jit(solution)/shard_map/while/body/eval_jaxpr/all_to_all | solution.py:78
  133.6 14.5 %all-to-all-start = ((bf16[16,2,32,128]{3,2,1,0:T(8,128)(2,1)}), bf16[16,2,32,128]{3,2,1,0:T(8,128)(2,1)S(1)}, u32[]{:S(2)}, u32[]{:S(2)}) async-start(bf16[16,2,32,128]{3,2,1,0:T(8,128)(2,1)} %broadcast_select_fusion.3), calls=%async_computation | async-start | bytes 524288 | tf_op jit(solution)/shard_map/while/body/eval_jaxpr/all_to_all | solution.py:78
  165.5 14.5 %all-to-all-start = ((bf16[16,2,32,128]{3,2,1,0:T(8,128)(2,1)}), bf16[16,2,32,128]{3,2,1,0:T(8,128)(2,1)S(1)}, u32[]{:S(2)}, u32[]{:S(2)}) async-start(bf16[16,2,32,128]{3,2,1,0:T(8,128)(2,1)} %broadcast_select_fusion.3), calls=%async_computation | async-start | bytes 524288 | tf_op jit(solution)/shard_map/while/body/eval_jaxpr/all_to_all | solution.py:78
  197.5 14.5 %all-to-all-start = ((bf16[16,2,32,128]{3,2,1,0:T(8,128)(2,1)}), bf16[16,2,32,128]{3,2,1,0:T(8,128)(2,1)S(1)}, u32[]{:S(2)}, u32[]{:S(2)}) async-start(bf16[16,2,32,128]{3,2,1,0:T(8,128)(2,1)} %broadcast_select_fusion.3), calls=%async_computation | async-start | bytes 524288 | tf_op jit(solution)/shard_map/while/body/eval_jaxpr/all_to_all | solution.py:78
  230.3 14.5 %all-to-all-start = ((bf16[16,2,32,128]{3,2,1,0:T(8,128)(2,1)}), bf16[16,2,32,128]{3,2,1,0:T(8,128)(2,1)S(1)}, u32[]{:S(2)}, u32[]{:S(2)}) async-start(bf16[16,2,32,128]{3,2,1,0:T(8,128)(2,1)} %broadcast_select_fusion.3), calls=%async_computation | async-start | bytes 524288 | tf_op jit(solution)/shard_map/while/body/eval_jaxpr/all_to_all | solution.py:78
  248.7 13.0 %collective-permute-start = (bf16[32,32,128]{2,1,0:T(8,128)(2,1)S(1)}, bf16[32,32,128]{2,1,0:T(8,128)(2,1)S(1)}, u32[]{:S(2)}, u32[]{:S(2)}) collective-permute-start(bf16[32,32,128]{2,1,0:T(8,128)(2,1)S(1)} %get-tuple-element.421), channel_id=1, source_target_pairs={{0,16},{16,32},{32,48},{48,64},{64,80},{80,96},{96,112},{112,128},... | collective-permute-start | bytes 786440 | tf_op jit(solution)/shard_map/while/body/eval_jaxpr/ppermute | solution.py:12
  264.3 14.5 %all-to-all-start = ((bf16[16,2,32,128]{3,2,1,0:T(8,128)(2,1)}), bf16[16,2,32,128]{3,2,1,0:T(8,128)(2,1)S(1)}, u32[]{:S(2)}, u32[]{:S(2)}) async-start(bf16[16,2,32,128]{3,2,1,0:T(8,128)(2,1)} %broadcast_select_fusion.3), calls=%async_computation | async-start | bytes 524288 | tf_op jit(solution)/shard_map/while/body/eval_jaxpr/all_to_all | solution.py:78
  282.7 13.0 %collective-permute-start = (bf16[32,32,128]{2,1,0:T(8,128)(2,1)S(1)}, bf16[32,32,128]{2,1,0:T(8,128)(2,1)S(1)}, u32[]{:S(2)}, u32[]{:S(2)}) collective-permute-start(bf16[32,32,128]{2,1,0:T(8,128)(2,1)S(1)} %get-tuple-element.421), channel_id=1, source_target_pairs={{0,16},{16,32},{32,48},{48,64},{64,80},{80,96},{96,112},{112,128},... | collective-permute-start | bytes 786440 | tf_op jit(solution)/shard_map/while/body/eval_jaxpr/ppermute | solution.py:12
  298.4 14.5 %all-to-all-start = ((bf16[16,2,32,128]{3,2,1,0:T(8,128)(2,1)}), bf16[16,2,32,128]{3,2,1,0:T(8,128)(2,1)S(1)}, u32[]{:S(2)}, u32[]{:S(2)}) async-start(bf16[16,2,32,128]{3,2,1,0:T(8,128)(2,1)} %broadcast_select_fusion.3), calls=%async_computation | async-start | bytes 524288 | tf_op jit(solution)/shard_map/while/body/eval_jaxpr/all_to_all | solution.py:78
  316.7 13.0 %collective-permute-start = (bf16[32,32,128]{2,1,0:T(8,128)(2,1)S(1)}, bf16[32,32,128]{2,1,0:T(8,128)(2,1)S(1)}, u32[]{:S(2)}, u32[]{:S(2)}) collective-permute-start(bf16[32,32,128]{2,1,0:T(8,128)(2,1)S(1)} %get-tuple-element.421), channel_id=1, source_target_pairs={{0,16},{16,32},{32,48},{48,64},{64,80},{80,96},{96,112},{112,128},... | collective-permute-start | bytes 786440 | tf_op jit(solution)/shard_map/while/body/eval_jaxpr/ppermute | solution.py:12
  332.4 14.5 %all-to-all-start = ((bf16[16,2,32,128]{3,2,1,0:T(8,128)(2,1)}), bf16[16,2,32,128]{3,2,1,0:T(8,128)(2,1)S(1)}, u32[]{:S(2)}, u32[]{:S(2)}) async-start(bf16[16,2,32,128]{3,2,1,0:T(8,128)(2,1)} %broadcast_select_fusion.3), calls=%async_computation | async-start | bytes 524288 | tf_op jit(solution)/shard_map/while/body/eval_jaxpr/all_to_all | solution.py:78
  350.8 13.0 %collective-permute-start = (bf16[32,32,128]{2,1,0:T(8,128)(2,1)S(1)}, bf16[32,32,128]{2,1,0:T(8,128)(2,1)S(1)}, u32[]{:S(2)}, u32[]{:S(2)}) collective-permute-start(bf16[32,32,128]{2,1,0:T(8,128)(2,1)S(1)} %get-tuple-element.421), channel_id=1, source_target_pairs={{0,16},{16,32},{32,48},{48,64},{64,80},{80,96},{96,112},{112,128},... | collective-permute-start | bytes 786440 | tf_op jit(solution)/shard_map/while/body/eval_jaxpr/ppermute | solution.py:12
  366.4 14.5 %all-to-all-start = ((bf16[16,2,32,128]{3,2,1,0:T(8,128)(2,1)}), bf16[16,2,32,128]{3,2,1,0:T(8,128)(2,1)S(1)}, u32[]{:S(2)}, u32[]{:S(2)}) async-start(bf16[16,2,32,128]{3,2,1,0:T(8,128)(2,1)} %broadcast_select_fusion.3), calls=%async_computation | async-start | bytes 524288 | tf_op jit(solution)/shard_map/while/body/eval_jaxpr/all_to_all | solution.py:78
  384.8 13.0 %collective-permute-start = (bf16[32,32,128]{2,1,0:T(8,128)(2,1)S(1)}, bf16[32,32,128]{2,1,0:T(8,128)(2,1)S(1)}, u32[]{:S(2)}, u32[]{:S(2)}) collective-permute-start(bf16[32,32,128]{2,1,0:T(8,128)(2,1)S(1)} %get-tuple-element.421), channel_id=1, source_target_pairs={{0,16},{16,32},{32,48},{48,64},{64,80},{80,96},{96,112},{112,128},... | collective-permute-start | bytes 786440 | tf_op jit(solution)/shard_map/while/body/eval_jaxpr/ppermute | solution.py:12
  400.5 14.5 %all-to-all-start = ((bf16[16,2,32,128]{3,2,1,0:T(8,128)(2,1)}), bf16[16,2,32,128]{3,2,1,0:T(8,128)(2,1)S(1)}, u32[]{:S(2)}, u32[]{:S(2)}) async-start(bf16[16,2,32,128]{3,2,1,0:T(8,128)(2,1)} %broadcast_select_fusion.3), calls=%async_computation | async-start | bytes 524288 | tf_op jit(solution)/shard_map/while/body/eval_jaxpr/all_to_all | solution.py:78
  418.9 13.0 %collective-permute-start = (bf16[32,32,128]{2,1,0:T(8,128)(2,1)S(1)}, bf16[32,32,128]{2,1,0:T(8,128)(2,1)S(1)}, u32[]{:S(2)}, u32[]{:S(2)}) collective-permute-start(bf16[32,32,128]{2,1,0:T(8,128)(2,1)S(1)} %get-tuple-element.421), channel_id=1, source_target_pairs={{0,16},{16,32},{32,48},{48,64},{64,80},{80,96},{96,112},{112,128},... | collective-permute-start | bytes 786440 | tf_op jit(solution)/shard_map/while/body/eval_jaxpr/ppermute | solution.py:12
  434.5 14.5 %all-to-all-start = ((bf16[16,2,32,128]{3,2,1,0:T(8,128)(2,1)}), bf16[16,2,32,128]{3,2,1,0:T(8,128)(2,1)S(1)}, u32[]{:S(2)}, u32[]{:S(2)}) async-start(bf16[16,2,32,128]{3,2,1,0:T(8,128)(2,1)} %broadcast_select_fusion.3), calls=%async_computation | async-start | bytes 524288 | tf_op jit(solution)/shard_map/while/body/eval_jaxpr/all_to_all | solution.py:78
  452.9 13.0 %collective-permute-start = (bf16[32,32,128]{2,1,0:T(8,128)(2,1)S(1)}, bf16[32,32,128]{2,1,0:T(8,128)(2,1)S(1)}, u32[]{:S(2)}, u32[]{:S(2)}) collective-permute-start(bf16[32,32,128]{2,1,0:T(8,128)(2,1)S(1)} %get-tuple-element.421), channel_id=1, source_target_pairs={{0,16},{16,32},{32,48},{48,64},{64,80},{80,96},{96,112},{112,128},... | collective-permute-start | bytes 786440 | tf_op jit(solution)/shard_map/while/body/eval_jaxpr/ppermute | solution.py:12
  468.5 14.5 %all-to-all-start = ((bf16[16,2,32,128]{3,2,1,0:T(8,128)(2,1)}), bf16[16,2,32,128]{3,2,1,0:T(8,128)(2,1)S(1)}, u32[]{:S(2)}, u32[]{:S(2)}) async-start(bf16[16,2,32,128]{3,2,1,0:T(8,128)(2,1)} %broadcast_select_fusion.3), calls=%async_computation | async-start | bytes 524288 | tf_op jit(solution)/shard_map/while/body/eval_jaxpr/all_to_all | solution.py:78
  486.9 13.0 %collective-permute-start = (bf16[32,32,128]{2,1,0:T(8,128)(2,1)S(1)}, bf16[32,32,128]{2,1,0:T(8,128)(2,1)S(1)}, u32[]{:S(2)}, u32[]{:S(2)}) collective-permute-start(bf16[32,32,128]{2,1,0:T(8,128)(2,1)S(1)} %get-tuple-element.421), channel_id=1, source_target_pairs={{0,16},{16,32},{32,48},{48,64},{64,80},{80,96},{96,112},{112,128},... | collective-permute-start | bytes 786440 | tf_op jit(solution)/shard_map/while/body/eval_jaxpr/ppermute | solution.py:12
  502.6 14.5 %all-to-all-start = ((bf16[16,2,32,128]{3,2,1,0:T(8,128)(2,1)}), bf16[16,2,32,128]{3,2,1,0:T(8,128)(2,1)S(1)}, u32[]{:S(2)}, u32[]{:S(2)}) async-start(bf16[16,2,32,128]{3,2,1,0:T(8,128)(2,1)} %broadcast_select_fusion.3), calls=%async_computation | async-start | bytes 524288 | tf_op jit(solution)/shard_map/while/body/eval_jaxpr/all_to_all | solution.py:78
  521.0 13.0 %collective-permute-start = (bf16[32,32,128]{2,1,0:T(8,128)(2,1)S(1)}, bf16[32,32,128]{2,1,0:T(8,128)(2,1)S(1)}, u32[]{:S(2)}, u32[]{:S(2)}) collective-permute-start(bf16[32,32,128]{2,1,0:T(8,128)(2,1)S(1)} %get-tuple-element.421), channel_id=1, source_target_pairs={{0,16},{16,32},{32,48},{48,64},{64,80},{80,96},{96,112},{112,128},... | collective-permute-start | bytes 786440 | tf_op jit(solution)/shard_map/while/body/eval_jaxpr/ppermute | solution.py:12
  536.6 14.5 %all-to-all-start = ((bf16[16,2,32,128]{3,2,1,0:T(8,128)(2,1)}), bf16[16,2,32,128]{3,2,1,0:T(8,128)(2,1)S(1)}, u32[]{:S(2)}, u32[]{:S(2)}) async-start(bf16[16,2,32,128]{3,2,1,0:T(8,128)(2,1)} %broadcast_select_fusion.3), calls=%async_computation | async-start | bytes 524288 | tf_op jit(solution)/shard_map/while/body/eval_jaxpr/all_to_all | solution.py:78
  570.7 14.5 %all-to-all-start = ((bf16[16,2,32,128]{3,2,1,0:T(8,128)(2,1)}), bf16[16,2,32,128]{3,2,1,0:T(8,128)(2,1)S(1)}, u32[]{:S(2)}, u32[]{:S(2)}) async-start(bf16[16,2,32,128]{3,2,1,0:T(8,128)(2,1)} %broadcast_select_fusion.3), calls=%async_computation | async-start | bytes 524288 | tf_op jit(solution)/shard_map/while/body/eval_jaxpr/all_to_all | solution.py:78
  589.0 13.0 %collective-permute-start = (bf16[32,32,128]{2,1,0:T(8,128)(2,1)S(1)}, bf16[32,32,128]{2,1,0:T(8,128)(2,1)S(1)}, u32[]{:S(2)}, u32[]{:S(2)}) collective-permute-start(bf16[32,32,128]{2,1,0:T(8,128)(2,1)S(1)} %get-tuple-element.421), channel_id=1, source_target_pairs={{0,16},{16,32},{32,48},{48,64},{64,80},{80,96},{96,112},{112,128},... | collective-permute-start | bytes 786440 | tf_op jit(solution)/shard_map/while/body/eval_jaxpr/ppermute | solution.py:12
  604.7 14.5 %all-to-all-start = ((bf16[16,2,32,128]{3,2,1,0:T(8,128)(2,1)}), bf16[16,2,32,128]{3,2,1,0:T(8,128)(2,1)S(1)}, u32[]{:S(2)}, u32[]{:S(2)}) async-start(bf16[16,2,32,128]{3,2,1,0:T(8,128)(2,1)} %broadcast_select_fusion.3), calls=%async_computation | async-start | bytes 524288 | tf_op jit(solution)/shard_map/while/body/eval_jaxpr/all_to_all | solution.py:78
  623.1 13.0 %collective-permute-start = (bf16[32,32,128]{2,1,0:T(8,128)(2,1)S(1)}, bf16[32,32,128]{2,1,0:T(8,128)(2,1)S(1)}, u32[]{:S(2)}, u32[]{:S(2)}) collective-permute-start(bf16[32,32,128]{2,1,0:T(8,128)(2,1)S(1)} %get-tuple-element.421), channel_id=1, source_target_pairs={{0,16},{16,32},{32,48},{48,64},{64,80},{80,96},{96,112},{112,128},... | collective-permute-start | bytes 786440 | tf_op jit(solution)/shard_map/while/body/eval_jaxpr/ppermute | solution.py:12
  638.7 14.5 %all-to-all-start = ((bf16[16,2,32,128]{3,2,1,0:T(8,128)(2,1)}), bf16[16,2,32,128]{3,2,1,0:T(8,128)(2,1)S(1)}, u32[]{:S(2)}, u32[]{:S(2)}) async-start(bf16[16,2,32,128]{3,2,1,0:T(8,128)(2,1)} %broadcast_select_fusion.3), calls=%async_computation | async-start | bytes 524288 | tf_op jit(solution)/shard_map/while/body/eval_jaxpr/all_to_all | solution.py:78
  672.8 14.5 %all-to-all-start = ((bf16[16,2,32,128]{3,2,1,0:T(8,128)(2,1)}), bf16[16,2,32,128]{3,2,1,0:T(8,128)(2,1)S(1)}, u32[]{:S(2)}, u32[]{:S(2)}) async-start(bf16[16,2,32,128]{3,2,1,0:T(8,128)(2,1)} %broadcast_select_fusion.3), calls=%async_computation | async-start | bytes 524288 | tf_op jit(solution)/shard_map/while/body/eval_jaxpr/all_to_all | solution.py:78
  707.0 31.1 %all-to-all-start.1 = ((bf16[4,16,2,4096]{3,2,0,1:T(2,128)(2,1)}), bf16[4,16,2,4096]{3,2,0,1:T(2,128)(2,1)S(1)}, u32[]{:S(2)}, u32[]{:S(2)}) async-start(bf16[4,16,2,4096]{3,2,0,1:T(2,128)(2,1)} %copy.26), calls=%async_computation.1 | async-start | bytes 2097152 | tf_op jit(solution)/shard_map/all_to_all | solution.py:107
  (10 other events, 168.4 us)
Sparse Core Ops, SparseCore 0:
  9.8 50.1 all-gather.2
where the time goes:
time: 750 us; the launch traced here: 746 us
  waiting for transfers between devices  371 us (49%)
  starting transfers between devices  194 us (26%)
  local copies, waits for them, and re-layouts  59.3 us (8%)
  matrix products  58.6 us (8%)
  other arithmetic  25.8 us (3%)
  blocking collectives  20.7 us (3%)
  between operations  13.5 us (2%)
    all_to_all x19, waiting for transfers between devices, apply_layer(): lax.all_to_all(payload, 'col', split_axis=0, concat_axis=0, tiled=True)  206 us
    ppermute x19, waiting for transfers between devices, from_behind(): return lax.ppermute(x, axis, pairs)  128 us
    ppermute x19, starting transfers between devices, from_behind(): return lax.ppermute(x, axis, pairs)  109 us
    all_to_all x19, starting transfers between devices, apply_layer(): lax.all_to_all(payload, 'col', split_axis=0, concat_axis=0, tiled=True)  70.7 us
    dot_general x19, matrix products, combine(): jnp.einsum('ckrb,ckbo->cro', picked, local_w, preferred_element_type=jnp....  58.6 us
    all_gather x1, waiting for transfers between devices, body(): all_inputs = lax.all_gather(features, 'section', axis=1, tiled=True)  21.1 us
    all_gather x1, blocking collectives, body(): pattern_table = lax.all_gather(sources[0], 'col', axis=0, tiled=True)  20.7 us
    dynamic_slice x19, local copies, waits for them, and re-layouts, tick(): lax.dynamic_index_in_dim(blocks_in, jnp.minimum(tick_idx, piece_total - 1...  18.6 us
  transfers between devices with their start and end apart: 40, of which 40 were waited for; matrix products, arithmetic and copies ran while one was open for 2% of the time, Pallas kernels for 0%

commit v1 on v0

--- a/solution.py
+++ b/solution.py
@@ -38,7 +38,22 @@
     block_size = local_w.shape[2]
     local_src = sources[0].reshape(blocks_own * nonzero_count)
     local_bias = bias[0].reshape(blocks_own, 1, block_size)
-    pattern_table = lax.all_gather(sources[0], "col", axis=0, tiled=True)
+    ways, here, step = (lax.axis_size("col"), lax.axis_index("col"), sources[0].shape[0])
+    shape = [n * ways if d == 0 else n for d, n in enumerate(sources[0].shape)]
+    pattern_table = lax.dynamic_update_slice_in_dim(
+        jnp.zeros(shape, sources[0].dtype), sources[0], here * step, axis=0
+    )
+    going_up = going_down = sources[0]
+    for far in range(1, ways // 2 + 1):
+        going_up = lax.ppermute(going_up, "col", [(d, (d + 1) % ways) for d in range(ways)])
+        pattern_table = lax.dynamic_update_slice_in_dim(
+            pattern_table, going_up, (here - far) % ways * step, axis=0
+        )
+        if 2 * far < ways:
+            going_down = lax.ppermute(going_down, "col", [(d, (d - 1) % ways) for d in range(ways)])
+            pattern_table = lax.dynamic_update_slice_in_dim(
+                pattern_table, going_down, (here + far) % ways * step, axis=0
+            )
     positions, present = request_lists(pattern_table, owners, blocks_own, CAP)
     outgoing = lax.dynamic_index_in_dim(positions, col_idx, 1, keepdims=False).reshape(owners * CAP)
     incoming = lax.dynamic_index_in_dim(positions, col_idx, 0, keepdims=False)

time: 750 us -> 749 us (level)
  starting transfers between devices: 194 us -> 217 us
  blocking collectives: 20.7 us -> 0 us
    ppermute x0 -> x15, starting transfers between devices: none -> 23.2 us  [the longest x7 23.1 us: body(): lax.ppermute(going_down, 'col', [(d, (d - 1) % ways) for d in range(ways)])]
    all_gather x1 -> x0, blocking collectives: 20.7 us -> none  [body(): pattern_table = lax.all_gather(sources[0], 'col', axis=0, tiled=True)]
    all_gather x1, waiting for transfers between devices: 21.1 us -> 7.39 us  [body(): all_inputs = lax.all_gather(features, 'section', axis=1, tiled=True)]
    ppermute x0 -> x15, waiting for transfers between devices: none -> 11.3 us  [the longest x8 10.2 us: body(): lax.ppermute(going_up, 'col', [(d, (d + 1) % ways) for d in range(ways)])]
  transfers between devices with their start and end apart: 40 -> 55, of which waited for: 40 -> 51; matrix products, arithmetic and copies ran while one was open for 2% -> 2% of each run, Pallas kernels for 0% -> 0%
where the time goes in v1:
time: 749 us; the launch traced here: 745 us
  waiting for transfers between devices  369 us (49%)
  starting transfers between devices  217 us (29%)
  local copies, waits for them, and re-layouts  60 us (8%)
  matrix products  58.6 us (8%)
  other arithmetic  24.3 us (3%)
  between operations  13.9 us (2%)
    all_to_all x19, waiting for transfers between devices, apply_layer(): lax.all_to_all(payload, 'col', split_axis=0, concat_axis=0, tiled=True)  206 us
    ppermute x19, waiting for transfers between devices, from_behind(): return lax.ppermute(x, axis, pairs)  128 us
    ppermute x19, starting transfers between devices, from_behind(): return lax.ppermute(x, axis, pairs)  109 us
    all_to_all x19, starting transfers between devices, apply_layer(): lax.all_to_all(payload, 'col', split_axis=0, concat_axis=0, tiled=True)  70.6 us
    dot_general x19, matrix products, combine(): jnp.einsum('ckrb,ckbo->cro', picked, local_w, preferred_element_type=jnp....  58.6 us
    ppermute x7, starting transfers between devices, body(): lax.ppermute(going_down, 'col', [(d, (d - 1) % ways) for d in range(ways)])  23.1 us
    dynamic_slice x19, local copies, waits for them, and re-layouts, tick(): lax.dynamic_index_in_dim(blocks_in, jnp.minimum(tick_idx, piece_total - 1...  18.6 us
    all_to_all x1, waiting for transfers between devices, body(): lax.all_to_all(outgoing_rows, 'section', split_axis=1, concat_axis=1, til...  16.6 us
  transfers between devices with their start and end apart: 55, of which 51 were waited for; matrix products, arithmetic and copies ran while one was open for 2% of the time, Pallas kernels for 0%

profile of v1, /device:TPU:8, one launch (start us, length us, event | category | flops | bytes accessed | tf_op | source)
XLA Modules:
  0.0 745.4 jit_solution(12340416438863014826)
XLA Ops:
  52.6 7.4 all-gather.2.cloned.1.call-done
  63.1 640.8 %while.19 = (s32[]{:T(128)}, bf16[32,32,128]{2,1,0:T(8,128)(2,1)S(1)}, bf16[4,32,32,128]{3,2,1,0:T(8,128)(2,1)S(1)}, s32[128]{0:T(128)S(1)}, s32[32]{0:T(128)S(1...) while((s32[]{:T(128)}, ...), condition=%wide.region_6.7_spmd, body=%wide.region_5.6_spmd.sunk | while | flops 135531952 | bytes 12878729 | solution.py:115
  65.8 7.1 all-to-all-start
  73.1 11.0 %all-to-all-done = bf16[16,2,32,128]{3,2,1,0:T(8,128)(2,1)S(1)} async-done(((bf16[16,2,32,128]{3,2,1,0:T(8,128)(2,1)}), bf16[16,2,32,128]{3,2,1,0:T(8,128)(2,1)S(1)}, u32[]{:S(2)}, u32[]{:S(2)}) %all-to-all-start) | async-done | bytes 262176 | tf_op jit(solution)/shard_map/while/body/eval_jaxpr/all_to_all | solution.py:93
  91.1 7.8 %collective-permute-done = bf16[32,32,128]{2,1,0:T(8,128)(2,1)S(1)} collective-permute-done((bf16[32,32,128]{2,1,0:T(8,128)(2,1)S(1)}, bf16[32,32,128]{2,1,0:T(8,128)(2,1)S(1)}, u32[]{:S(2)}, u32[]{:S(2)}) %collective-permute-start) | collective-permute-done | bytes 262176 | tf_op jit(solution)/shard_map/while/body/eval_jaxpr/ppermute | solution.py:12
  105.3 10.8 %all-to-all-done = bf16[16,2,32,128]{3,2,1,0:T(8,128)(2,1)S(1)} async-done(((bf16[16,2,32,128]{3,2,1,0:T(8,128)(2,1)}), bf16[16,2,32,128]{3,2,1,0:T(8,128)(2,1)S(1)}, u32[]{:S(2)}, u32[]{:S(2)}) %all-to-all-start) | async-done | bytes 262176 | tf_op jit(solution)/shard_map/while/body/eval_jaxpr/all_to_all | solution.py:93
  123.2 7.7 %collective-permute-done = bf16[32,32,128]{2,1,0:T(8,128)(2,1)S(1)} collective-permute-done((bf16[32,32,128]{2,1,0:T(8,128)(2,1)S(1)}, bf16[32,32,128]{2,1,0:T(8,128)(2,1)S(1)}, u32[]{:S(2)}, u32[]{:S(2)}) %collective-permute-start) | collective-permute-done | bytes 262176 | tf_op jit(solution)/shard_map/while/body/eval_jaxpr/ppermute | solution.py:12
  137.2 10.8 %all-to-all-done = bf16[16,2,32,128]{3,2,1,0:T(8,128)(2,1)S(1)} async-done(((bf16[16,2,32,128]{3,2,1,0:T(8,128)(2,1)}), bf16[16,2,32,128]{3,2,1,0:T(8,128)(2,1)S(1)}, u32[]{:S(2)}, u32[]{:S(2)}) %all-to-all-start) | async-done | bytes 262176 | tf_op jit(solution)/shard_map/while/body/eval_jaxpr/all_to_all | solution.py:93
  155.1 7.7 %collective-permute-done = bf16[32,32,128]{2,1,0:T(8,128)(2,1)S(1)} collective-permute-done((bf16[32,32,128]{2,1,0:T(8,128)(2,1)S(1)}, bf16[32,32,128]{2,1,0:T(8,128)(2,1)S(1)}, u32[]{:S(2)}, u32[]{:S(2)}) %collective-permute-start) | collective-permute-done | bytes 262176 | tf_op jit(solution)/shard_map/while/body/eval_jaxpr/ppermute | solution.py:12
  169.1 10.8 %all-to-all-done = bf16[16,2,32,128]{3,2,1,0:T(8,128)(2,1)S(1)} async-done(((bf16[16,2,32,128]{3,2,1,0:T(8,128)(2,1)}), bf16[16,2,32,128]{3,2,1,0:T(8,128)(2,1)S(1)}, u32[]{:S(2)}, u32[]{:S(2)}) %all-to-all-start) | async-done | bytes 262176 | tf_op jit(solution)/shard_map/while/body/eval_jaxpr/all_to_all | solution.py:93
  187.0 7.6 %collective-permute-done = bf16[32,32,128]{2,1,0:T(8,128)(2,1)S(1)} collective-permute-done((bf16[32,32,128]{2,1,0:T(8,128)(2,1)S(1)}, bf16[32,32,128]{2,1,0:T(8,128)(2,1)S(1)}, u32[]{:S(2)}, u32[]{:S(2)}) %collective-permute-start) | collective-permute-done | bytes 262176 | tf_op jit(solution)/shard_map/while/body/eval_jaxpr/ppermute | solution.py:12
  201.1 10.8 %all-to-all-done = bf16[16,2,32,128]{3,2,1,0:T(8,128)(2,1)S(1)} async-done(((bf16[16,2,32,128]{3,2,1,0:T(8,128)(2,1)}), bf16[16,2,32,128]{3,2,1,0:T(8,128)(2,1)S(1)}, u32[]{:S(2)}, u32[]{:S(2)}) %all-to-all-start) | async-done | bytes 262176 | tf_op jit(solution)/shard_map/while/body/eval_jaxpr/all_to_all | solution.py:93
  233.9 10.8 %all-to-all-done = bf16[16,2,32,128]{3,2,1,0:T(8,128)(2,1)S(1)} async-done(((bf16[16,2,32,128]{3,2,1,0:T(8,128)(2,1)}), bf16[16,2,32,128]{3,2,1,0:T(8,128)(2,1)S(1)}, u32[]{:S(2)}, u32[]{:S(2)}) %all-to-all-start) | async-done | bytes 262176 | tf_op jit(solution)/shard_map/while/body/eval_jaxpr/all_to_all | solution.py:93
  248.5 6.5 collective-permute-start
  267.9 10.8 %all-to-all-done = bf16[16,2,32,128]{3,2,1,0:T(8,128)(2,1)S(1)} async-done(((bf16[16,2,32,128]{3,2,1,0:T(8,128)(2,1)}), bf16[16,2,32,128]{3,2,1,0:T(8,128)(2,1)S(1)}, u32[]{:S(2)}, u32[]{:S(2)}) %all-to-all-start) | async-done | bytes 262176 | tf_op jit(solution)/shard_map/while/body/eval_jaxpr/all_to_all | solution.py:93
  282.6 6.5 collective-permute-start
  301.9 10.8 %all-to-all-done = bf16[16,2,32,128]{3,2,1,0:T(8,128)(2,1)S(1)} async-done(((bf16[16,2,32,128]{3,2,1,0:T(8,128)(2,1)}), bf16[16,2,32,128]{3,2,1,0:T(8,128)(2,1)S(1)}, u32[]{:S(2)}, u32[]{:S(2)}) %all-to-all-start) | async-done | bytes 262176 | tf_op jit(solution)/shard_map/while/body/eval_jaxpr/all_to_all | solution.py:93
  316.6 6.5 collective-permute-start
  336.0 10.8 %all-to-all-done = bf16[16,2,32,128]{3,2,1,0:T(8,128)(2,1)S(1)} async-done(((bf16[16,2,32,128]{3,2,1,0:T(8,128)(2,1)}), bf16[16,2,32,128]{3,2,1,0:T(8,128)(2,1)S(1)}, u32[]{:S(2)}, u32[]{:S(2)}) %all-to-all-start) | async-done | bytes 262176 | tf_op jit(solution)/shard_map/while/body/eval_jaxpr/all_to_all | solution.py:93
  350.6 6.5 collective-permute-start
  370.0 10.8 %all-to-all-done = bf16[16,2,32,128]{3,2,1,0:T(8,128)(2,1)S(1)} async-done(((bf16[16,2,32,128]{3,2,1,0:T(8,128)(2,1)}), bf16[16,2,32,128]{3,2,1,0:T(8,128)(2,1)S(1)}, u32[]{:S(2)}, u32[]{:S(2)}) %all-to-all-start) | async-done | bytes 262176 | tf_op jit(solution)/shard_map/while/body/eval_jaxpr/all_to_all | solution.py:93
  404.0 10.8 %all-to-all-done = bf16[16,2,32,128]{3,2,1,0:T(8,128)(2,1)S(1)} async-done(((bf16[16,2,32,128]{3,2,1,0:T(8,128)(2,1)}), bf16[16,2,32,128]{3,2,1,0:T(8,128)(2,1)S(1)}, u32[]{:S(2)}, u32[]{:S(2)}) %all-to-all-start) | async-done | bytes 262176 | tf_op jit(solution)/shard_map/while/body/eval_jaxpr/all_to_all | solution.py:93
  438.0 10.8 %all-to-all-done = bf16[16,2,32,128]{3,2,1,0:T(8,128)(2,1)S(1)} async-done(((bf16[16,2,32,128]{3,2,1,0:T(8,128)(2,1)}), bf16[16,2,32,128]{3,2,1,0:T(8,128)(2,1)S(1)}, u32[]{:S(2)}, u32[]{:S(2)}) %all-to-all-start) | async-done | bytes 262176 | tf_op jit(solution)/shard_map/while/body/eval_jaxpr/all_to_all | solution.py:93
  472.1 10.8 %all-to-all-done = bf16[16,2,32,128]{3,2,1,0:T(8,128)(2,1)S(1)} async-done(((bf16[16,2,32,128]{3,2,1,0:T(8,128)(2,1)}), bf16[16,2,32,128]{3,2,1,0:T(8,128)(2,1)S(1)}, u32[]{:S(2)}, u32[]{:S(2)}) %all-to-all-start) | async-done | bytes 262176 | tf_op jit(solution)/shard_map/while/body/eval_jaxpr/all_to_all | solution.py:93
  506.1 10.8 %all-to-all-done = bf16[16,2,32,128]{3,2,1,0:T(8,128)(2,1)S(1)} async-done(((bf16[16,2,32,128]{3,2,1,0:T(8,128)(2,1)}), bf16[16,2,32,128]{3,2,1,0:T(8,128)(2,1)S(1)}, u32[]{:S(2)}, u32[]{:S(2)}) %all-to-all-start) | async-done | bytes 262176 | tf_op jit(solution)/shard_map/while/body/eval_jaxpr/all_to_all | solution.py:93
  540.1 10.8 %all-to-all-done = bf16[16,2,32,128]{3,2,1,0:T(8,128)(2,1)S(1)} async-done(((bf16[16,2,32,128]{3,2,1,0:T(8,128)(2,1)}), bf16[16,2,32,128]{3,2,1,0:T(8,128)(2,1)S(1)}, u32[]{:S(2)}, u32[]{:S(2)}) %all-to-all-start) | async-done | bytes 262176 | tf_op jit(solution)/shard_map/while/body/eval_jaxpr/all_to_all | solution.py:93
  574.2 10.8 %all-to-all-done = bf16[16,2,32,128]{3,2,1,0:T(8,128)(2,1)S(1)} async-done(((bf16[16,2,32,128]{3,2,1,0:T(8,128)(2,1)}), bf16[16,2,32,128]{3,2,1,0:T(8,128)(2,1)S(1)}, u32[]{:S(2)}, u32[]{:S(2)}) %all-to-all-start) | async-done | bytes 262176 | tf_op jit(solution)/shard_map/while/body/eval_jaxpr/all_to_all | solution.py:93
  608.2 10.8 %all-to-all-done = bf16[16,2,32,128]{3,2,1,0:T(8,128)(2,1)S(1)} async-done(((bf16[16,2,32,128]{3,2,1,0:T(8,128)(2,1)}), bf16[16,2,32,128]{3,2,1,0:T(8,128)(2,1)S(1)}, u32[]{:S(2)}, u32[]{:S(2)}) %all-to-all-start) | async-done | bytes 262176 | tf_op jit(solution)/shard_map/while/body/eval_jaxpr/all_to_all | solution.py:93
  642.2 10.8 %all-to-all-done = bf16[16,2,32,128]{3,2,1,0:T(8,128)(2,1)S(1)} async-done(((bf16[16,2,32,128]{3,2,1,0:T(8,128)(2,1)}), bf16[16,2,32,128]{3,2,1,0:T(8,128)(2,1)S(1)}, u32[]{:S(2)}, u32[]{:S(2)}) %all-to-all-start) | async-done | bytes 262176 | tf_op jit(solution)/shard_map/while/body/eval_jaxpr/all_to_all | solution.py:93
  676.2 10.8 %all-to-all-done = bf16[16,2,32,128]{3,2,1,0:T(8,128)(2,1)S(1)} async-done(((bf16[16,2,32,128]{3,2,1,0:T(8,128)(2,1)}), bf16[16,2,32,128]{3,2,1,0:T(8,128)(2,1)S(1)}, u32[]{:S(2)}, u32[]{:S(2)}) %all-to-all-start) | async-done | bytes 262176 | tf_op jit(solution)/shard_map/while/body/eval_jaxpr/all_to_all | solution.py:93
  706.8 14.3 %all-to-all-start.1 = ((bf16[4,16,2,4096]{3,2,0,1:T(2,128)(2,1)}), bf16[4,16,2,4096]{3,2,0,1:T(2,128)(2,1)S(1)}, u32[]{:S(2)}, u32[]{:S(2)}) async-start(bf16[4,16,2,4096]{3,2,0,1:T(2,128)(2,1)} %copy.71), calls=%async_computation.1 | async-start | bytes 2097152 | tf_op jit(solution)/shard_map/all_to_all | solution.py:122
  721.2 16.6 %all-to-all-done.1 = bf16[4,16,2,4096]{3,2,0,1:T(2,128)(2,1)S(1)} async-done(((bf16[4,16,2,4096]{3,2,0,1:T(2,128)(2,1)}), bf16[4,16,2,4096]{3,2,0,1:T(2,128)(2,1)S(1)}, u32[]{:S(2)}, u32[]{:S(2)}) %all-to-all-start.1) | async-done | bytes 1048608 | tf_op jit(solution)/shard_map/all_to_all | solution.py:122
  (435 shorter events, 421.6 us)
Async XLA Ops:
  6.5 53.5 %all-gather.2.cloned.1.call-start = ((), (), s32[]{:S(2)}) async-start(), calls=%async_computation.2 | async-start | bytes 1114112 | tf_op jit(solution)/shard_map/all_gather | solution.py:68
  65.8 18.3 %all-to-all-start = ((bf16[16,2,32,128]{3,2,1,0:T(8,128)(2,1)}), bf16[16,2,32,128]{3,2,1,0:T(8,128)(2,1)S(1)}, u32[]{:S(2)}, u32[]{:S(2)}) async-start(bf16[16,2,32,128]{3,2,1,0:T(8,128)(2,1)} %broadcast_select_fusion.3), calls=%async_computation | async-start | bytes 524288 | tf_op jit(solution)/shard_map/while/body/eval_jaxpr/all_to_all | solution.py:93
  101.6 14.5 %all-to-all-start = ((bf16[16,2,32,128]{3,2,1,0:T(8,128)(2,1)}), bf16[16,2,32,128]{3,2,1,0:T(8,128)(2,1)S(1)}, u32[]{:S(2)}, u32[]{:S(2)}) async-start(bf16[16,2,32,128]{3,2,1,0:T(8,128)(2,1)} %broadcast_select_fusion.3), calls=%async_computation | async-start | bytes 524288 | tf_op jit(solution)/shard_map/while/body/eval_jaxpr/all_to_all | solution.py:93
  133.5 14.5 %all-to-all-start = ((bf16[16,2,32,128]{3,2,1,0:T(8,128)(2,1)}), bf16[16,2,32,128]{3,2,1,0:T(8,128)(2,1)S(1)}, u32[]{:S(2)}, u32[]{:S(2)}) async-start(bf16[16,2,32,128]{3,2,1,0:T(8,128)(2,1)} %broadcast_select_fusion.3), calls=%async_computation | async-start | bytes 524288 | tf_op jit(solution)/shard_map/while/body/eval_jaxpr/all_to_all | solution.py:93
  165.4 14.5 %all-to-all-start = ((bf16[16,2,32,128]{3,2,1,0:T(8,128)(2,1)}), bf16[16,2,32,128]{3,2,1,0:T(8,128)(2,1)S(1)}, u32[]{:S(2)}, u32[]{:S(2)}) async-start(bf16[16,2,32,128]{3,2,1,0:T(8,128)(2,1)} %broadcast_select_fusion.3), calls=%async_computation | async-start | bytes 524288 | tf_op jit(solution)/shard_map/while/body/eval_jaxpr/all_to_all | solution.py:93
  197.3 14.5 %all-to-all-start = ((bf16[16,2,32,128]{3,2,1,0:T(8,128)(2,1)}), bf16[16,2,32,128]{3,2,1,0:T(8,128)(2,1)S(1)}, u32[]{:S(2)}, u32[]{:S(2)}) async-start(bf16[16,2,32,128]{3,2,1,0:T(8,128)(2,1)} %broadcast_select_fusion.3), calls=%async_computation | async-start | bytes 524288 | tf_op jit(solution)/shard_map/while/body/eval_jaxpr/all_to_all | solution.py:93
  230.1 14.5 %all-to-all-start = ((bf16[16,2,32,128]{3,2,1,0:T(8,128)(2,1)}), bf16[16,2,32,128]{3,2,1,0:T(8,128)(2,1)S(1)}, u32[]{:S(2)}, u32[]{:S(2)}) async-start(bf16[16,2,32,128]{3,2,1,0:T(8,128)(2,1)} %broadcast_select_fusion.3), calls=%async_computation | async-start | bytes 524288 | tf_op jit(solution)/shard_map/while/body/eval_jaxpr/all_to_all | solution.py:93
  248.5 13.0 %collective-permute-start = (bf16[32,32,128]{2,1,0:T(8,128)(2,1)S(1)}, bf16[32,32,128]{2,1,0:T(8,128)(2,1)S(1)}, u32[]{:S(2)}, u32[]{:S(2)}) collective-permute-start(bf16[32,32,128]{2,1,0:T(8,128)(2,1)S(1)} %get-tuple-element.421), channel_id=1, source_target_pairs={{0,16},{16,32},{32,48},{48,64},{64,80},{80,96},{96,112},{112,128},... | collective-permute-start | bytes 786440 | tf_op jit(solution)/shard_map/while/body/eval_jaxpr/ppermute | solution.py:12
  264.2 14.5 %all-to-all-start = ((bf16[16,2,32,128]{3,2,1,0:T(8,128)(2,1)}), bf16[16,2,32,128]{3,2,1,0:T(8,128)(2,1)S(1)}, u32[]{:S(2)}, u32[]{:S(2)}) async-start(bf16[16,2,32,128]{3,2,1,0:T(8,128)(2,1)} %broadcast_select_fusion.3), calls=%async_computation | async-start | bytes 524288 | tf_op jit(solution)/shard_map/while/body/eval_jaxpr/all_to_all | solution.py:93
  282.6 13.0 %collective-permute-start = (bf16[32,32,128]{2,1,0:T(8,128)(2,1)S(1)}, bf16[32,32,128]{2,1,0:T(8,128)(2,1)S(1)}, u32[]{:S(2)}, u32[]{:S(2)}) collective-permute-start(bf16[32,32,128]{2,1,0:T(8,128)(2,1)S(1)} %get-tuple-element.421), channel_id=1, source_target_pairs={{0,16},{16,32},{32,48},{48,64},{64,80},{80,96},{96,112},{112,128},... | collective-permute-start | bytes 786440 | tf_op jit(solution)/shard_map/while/body/eval_jaxpr/ppermute | solution.py:12
  298.2 14.5 %all-to-all-start = ((bf16[16,2,32,128]{3,2,1,0:T(8,128)(2,1)}), bf16[16,2,32,128]{3,2,1,0:T(8,128)(2,1)S(1)}, u32[]{:S(2)}, u32[]{:S(2)}) async-start(bf16[16,2,32,128]{3,2,1,0:T(8,128)(2,1)} %broadcast_select_fusion.3), calls=%async_computation | async-start | bytes 524288 | tf_op jit(solution)/shard_map/while/body/eval_jaxpr/all_to_all | solution.py:93
  316.6 13.0 %collective-permute-start = (bf16[32,32,128]{2,1,0:T(8,128)(2,1)S(1)}, bf16[32,32,128]{2,1,0:T(8,128)(2,1)S(1)}, u32[]{:S(2)}, u32[]{:S(2)}) collective-permute-start(bf16[32,32,128]{2,1,0:T(8,128)(2,1)S(1)} %get-tuple-element.421), channel_id=1, source_target_pairs={{0,16},{16,32},{32,48},{48,64},{64,80},{80,96},{96,112},{112,128},... | collective-permute-start | bytes 786440 | tf_op jit(solution)/shard_map/while/body/eval_jaxpr/ppermute | solution.py:12
  332.2 14.5 %all-to-all-start = ((bf16[16,2,32,128]{3,2,1,0:T(8,128)(2,1)}), bf16[16,2,32,128]{3,2,1,0:T(8,128)(2,1)S(1)}, u32[]{:S(2)}, u32[]{:S(2)}) async-start(bf16[16,2,32,128]{3,2,1,0:T(8,128)(2,1)} %broadcast_select_fusion.3), calls=%async_computation | async-start | bytes 524288 | tf_op jit(solution)/shard_map/while/body/eval_jaxpr/all_to_all | solution.py:93
  350.6 13.0 %collective-permute-start = (bf16[32,32,128]{2,1,0:T(8,128)(2,1)S(1)}, bf16[32,32,128]{2,1,0:T(8,128)(2,1)S(1)}, u32[]{:S(2)}, u32[]{:S(2)}) collective-permute-start(bf16[32,32,128]{2,1,0:T(8,128)(2,1)S(1)} %get-tuple-element.421), channel_id=1, source_target_pairs={{0,16},{16,32},{32,48},{48,64},{64,80},{80,96},{96,112},{112,128},... | collective-permute-start | bytes 786440 | tf_op jit(solution)/shard_map/while/body/eval_jaxpr/ppermute | solution.py:12
  366.3 14.5 %all-to-all-start = ((bf16[16,2,32,128]{3,2,1,0:T(8,128)(2,1)}), bf16[16,2,32,128]{3,2,1,0:T(8,128)(2,1)S(1)}, u32[]{:S(2)}, u32[]{:S(2)}) async-start(bf16[16,2,32,128]{3,2,1,0:T(8,128)(2,1)} %broadcast_select_fusion.3), calls=%async_computation | async-start | bytes 524288 | tf_op jit(solution)/shard_map/while/body/eval_jaxpr/all_to_all | solution.py:93
  384.6 13.0 %collective-permute-start = (bf16[32,32,128]{2,1,0:T(8,128)(2,1)S(1)}, bf16[32,32,128]{2,1,0:T(8,128)(2,1)S(1)}, u32[]{:S(2)}, u32[]{:S(2)}) collective-permute-start(bf16[32,32,128]{2,1,0:T(8,128)(2,1)S(1)} %get-tuple-element.421), channel_id=1, source_target_pairs={{0,16},{16,32},{32,48},{48,64},{64,80},{80,96},{96,112},{112,128},... | collective-permute-start | bytes 786440 | tf_op jit(solution)/shard_map/while/body/eval_jaxpr/ppermute | solution.py:12
  400.3 14.5 %all-to-all-start = ((bf16[16,2,32,128]{3,2,1,0:T(8,128)(2,1)}), bf16[16,2,32,128]{3,2,1,0:T(8,128)(2,1)S(1)}, u32[]{:S(2)}, u32[]{:S(2)}) async-start(bf16[16,2,32,128]{3,2,1,0:T(8,128)(2,1)} %broadcast_select_fusion.3), calls=%async_computation | async-start | bytes 524288 | tf_op jit(solution)/shard_map/while/body/eval_jaxpr/all_to_all | solution.py:93
  418.7 13.0 %collective-permute-start = (bf16[32,32,128]{2,1,0:T(8,128)(2,1)S(1)}, bf16[32,32,128]{2,1,0:T(8,128)(2,1)S(1)}, u32[]{:S(2)}, u32[]{:S(2)}) collective-permute-start(bf16[32,32,128]{2,1,0:T(8,128)(2,1)S(1)} %get-tuple-element.421), channel_id=1, source_target_pairs={{0,16},{16,32},{32,48},{48,64},{64,80},{80,96},{96,112},{112,128},... | collective-permute-start | bytes 786440 | tf_op jit(solution)/shard_map/while/body/eval_jaxpr/ppermute | solution.py:12
  434.3 14.5 %all-to-all-start = ((bf16[16,2,32,128]{3,2,1,0:T(8,128)(2,1)}), bf16[16,2,32,128]{3,2,1,0:T(8,128)(2,1)S(1)}, u32[]{:S(2)}, u32[]{:S(2)}) async-start(bf16[16,2,32,128]{3,2,1,0:T(8,128)(2,1)} %broadcast_select_fusion.3), calls=%async_computation | async-start | bytes 524288 | tf_op jit(solution)/shard_map/while/body/eval_jaxpr/all_to_all | solution.py:93
  452.7 13.0 %collective-permute-start = (bf16[32,32,128]{2,1,0:T(8,128)(2,1)S(1)}, bf16[32,32,128]{2,1,0:T(8,128)(2,1)S(1)}, u32[]{:S(2)}, u32[]{:S(2)}) collective-permute-start(bf16[32,32,128]{2,1,0:T(8,128)(2,1)S(1)} %get-tuple-element.421), channel_id=1, source_target_pairs={{0,16},{16,32},{32,48},{48,64},{64,80},{80,96},{96,112},{112,128},... | collective-permute-start | bytes 786440 | tf_op jit(solution)/shard_map/while/body/eval_jaxpr/ppermute | solution.py:12
  468.3 14.5 %all-to-all-start = ((bf16[16,2,32,128]{3,2,1,0:T(8,128)(2,1)}), bf16[16,2,32,128]{3,2,1,0:T(8,128)(2,1)S(1)}, u32[]{:S(2)}, u32[]{:S(2)}) async-start(bf16[16,2,32,128]{3,2,1,0:T(8,128)(2,1)} %broadcast_select_fusion.3), calls=%async_computation | async-start | bytes 524288 | tf_op jit(solution)/shard_map/while/body/eval_jaxpr/all_to_all | solution.py:93
  486.7 13.0 %collective-permute-start = (bf16[32,32,128]{2,1,0:T(8,128)(2,1)S(1)}, bf16[32,32,128]{2,1,0:T(8,128)(2,1)S(1)}, u32[]{:S(2)}, u32[]{:S(2)}) collective-permute-start(bf16[32,32,128]{2,1,0:T(8,128)(2,1)S(1)} %get-tuple-element.421), channel_id=1, source_target_pairs={{0,16},{16,32},{32,48},{48,64},{64,80},{80,96},{96,112},{112,128},... | collective-permute-start | bytes 786440 | tf_op jit(solution)/shard_map/while/body/eval_jaxpr/ppermute | solution.py:12
  502.4 14.5 %all-to-all-start = ((bf16[16,2,32,128]{3,2,1,0:T(8,128)(2,1)}), bf16[16,2,32,128]{3,2,1,0:T(8,128)(2,1)S(1)}, u32[]{:S(2)}, u32[]{:S(2)}) async-start(bf16[16,2,32,128]{3,2,1,0:T(8,128)(2,1)} %broadcast_select_fusion.3), calls=%async_computation | async-start | bytes 524288 | tf_op jit(solution)/shard_map/while/body/eval_jaxpr/all_to_all | solution.py:93
  520.8 13.0 %collective-permute-start = (bf16[32,32,128]{2,1,0:T(8,128)(2,1)S(1)}, bf16[32,32,128]{2,1,0:T(8,128)(2,1)S(1)}, u32[]{:S(2)}, u32[]{:S(2)}) collective-permute-start(bf16[32,32,128]{2,1,0:T(8,128)(2,1)S(1)} %get-tuple-element.421), channel_id=1, source_target_pairs={{0,16},{16,32},{32,48},{48,64},{64,80},{80,96},{96,112},{112,128},... | collective-permute-start | bytes 786440 | tf_op jit(solution)/shard_map/while/body/eval_jaxpr/ppermute | solution.py:12
  536.4 14.5 %all-to-all-start = ((bf16[16,2,32,128]{3,2,1,0:T(8,128)(2,1)}), bf16[16,2,32,128]{3,2,1,0:T(8,128)(2,1)S(1)}, u32[]{:S(2)}, u32[]{:S(2)}) async-start(bf16[16,2,32,128]{3,2,1,0:T(8,128)(2,1)} %broadcast_select_fusion.3), calls=%async_computation | async-start | bytes 524288 | tf_op jit(solution)/shard_map/while/body/eval_jaxpr/all_to_all | solution.py:93
  554.8 13.0 %collective-permute-start = (bf16[32,32,128]{2,1,0:T(8,128)(2,1)S(1)}, bf16[32,32,128]{2,1,0:T(8,128)(2,1)S(1)}, u32[]{:S(2)}, u32[]{:S(2)}) collective-permute-start(bf16[32,32,128]{2,1,0:T(8,128)(2,1)S(1)} %get-tuple-element.421), channel_id=1, source_target_pairs={{0,16},{16,32},{32,48},{48,64},{64,80},{80,96},{96,112},{112,128},... | collective-permute-start | bytes 786440 | tf_op jit(solution)/shard_map/while/body/eval_jaxpr/ppermute | solution.py:12
  570.4 14.5 %all-to-all-start = ((bf16[16,2,32,128]{3,2,1,0:T(8,128)(2,1)}), bf16[16,2,32,128]{3,2,1,0:T(8,128)(2,1)S(1)}, u32[]{:S(2)}, u32[]{:S(2)}) async-start(bf16[16,2,32,128]{3,2,1,0:T(8,128)(2,1)} %broadcast_select_fusion.3), calls=%async_computation | async-start | bytes 524288 | tf_op jit(solution)/shard_map/while/body/eval_jaxpr/all_to_all | solution.py:93
  604.5 14.5 %all-to-all-start = ((bf16[16,2,32,128]{3,2,1,0:T(8,128)(2,1)}), bf16[16,2,32,128]{3,2,1,0:T(8,128)(2,1)S(1)}, u32[]{:S(2)}, u32[]{:S(2)}) async-start(bf16[16,2,32,128]{3,2,1,0:T(8,128)(2,1)} %broadcast_select_fusion.3), calls=%async_computation | async-start | bytes 524288 | tf_op jit(solution)/shard_map/while/body/eval_jaxpr/all_to_all | solution.py:93
  622.9 13.0 %collective-permute-start = (bf16[32,32,128]{2,1,0:T(8,128)(2,1)S(1)}, bf16[32,32,128]{2,1,0:T(8,128)(2,1)S(1)}, u32[]{:S(2)}, u32[]{:S(2)}) collective-permute-start(bf16[32,32,128]{2,1,0:T(8,128)(2,1)S(1)} %get-tuple-element.421), channel_id=1, source_target_pairs={{0,16},{16,32},{32,48},{48,64},{64,80},{80,96},{96,112},{112,128},... | collective-permute-start | bytes 786440 | tf_op jit(solution)/shard_map/while/body/eval_jaxpr/ppermute | solution.py:12
  638.5 14.5 %all-to-all-start = ((bf16[16,2,32,128]{3,2,1,0:T(8,128)(2,1)}), bf16[16,2,32,128]{3,2,1,0:T(8,128)(2,1)S(1)}, u32[]{:S(2)}, u32[]{:S(2)}) async-start(bf16[16,2,32,128]{3,2,1,0:T(8,128)(2,1)} %broadcast_select_fusion.3), calls=%async_computation | async-start | bytes 524288 | tf_op jit(solution)/shard_map/while/body/eval_jaxpr/all_to_all | solution.py:93
  672.5 14.5 %all-to-all-start = ((bf16[16,2,32,128]{3,2,1,0:T(8,128)(2,1)}), bf16[16,2,32,128]{3,2,1,0:T(8,128)(2,1)S(1)}, u32[]{:S(2)}, u32[]{:S(2)}) async-start(bf16[16,2,32,128]{3,2,1,0:T(8,128)(2,1)} %broadcast_select_fusion.3), calls=%async_computation | async-start | bytes 524288 | tf_op jit(solution)/shard_map/while/body/eval_jaxpr/all_to_all | solution.py:93
  706.8 31.1 %all-to-all-start.1 = ((bf16[4,16,2,4096]{3,2,0,1:T(2,128)(2,1)}), bf16[4,16,2,4096]{3,2,0,1:T(2,128)(2,1)S(1)}, u32[]{:S(2)}, u32[]{:S(2)}) async-start(bf16[4,16,2,4096]{3,2,0,1:T(2,128)(2,1)} %copy.71), calls=%async_computation.1 | async-start | bytes 2097152 | tf_op jit(solution)/shard_map/all_to_all | solution.py:122
  (25 other events, 237.8 us)
Sparse Core Ops, SparseCore 0:
  13.5 46.4 all-gather.1
